TPU v7x, 256 devices: a whole 4x4x8 slice. The times are simulated.
256 devices in a mesh: req: 32 (over y, x, core), head: 8 (over z).
Axes of the slice: x: 4, y: 4, z: 8, core: 2. Of those that a mesh axis runs over, the one named last changes fastest.
Arguments:
- queries: bfloat16 [1024, 16384], P(('req', 'head')), may hold values from -15 to 15
- cache_keys: bfloat16 [8, 32768, 1024], P(None, 'req', 'head'), may hold values from -6 to 6
- cache_values: bfloat16 [8, 32768, 1024], P(None, 'req', 'head'), may hold values from -6 to 6
- tree_keys: bfloat16 [1024, 1024], P('req', 'head'), may hold values from -10 to 10
- tree_values: bfloat16 [1024, 1024], P('req', 'head'), may hold values from -6 to 6
- parents: int32 [8, 128], replicated, may hold values from -1 to 126, as said below
- tree_sizes: int32 [8], replicated, may hold values from 16 to 128
- cache_lens: int32 [8], replicated, may hold values from 2 to 32768
Outputs:
- attended: bfloat16 [1024, 16384], P('req', 'head')
Inputs may be any that keep to these rules, and one draw needn't show every extreme that they name: parents[a, 0] = -1 (the root); for node i >= 1, parents[a, i] is a node of 0 to i - 1.
All inputs are finite; a program needn't handle non-finite values.
Results may differ from a plain program's by a relative error of at most 0.003.
Values may be sent and summed in bfloat16 or wider, within the bound.
A program may use at most 128 MiB of HBM per device.

v0:
```python
import math
import jax
import jax.numpy as jnp
from jax import lax
from jax.sharding import Mesh
from jax.sharding import PartitionSpec as P

NH = 128
KVH = 8
HD = 128
negative_fill = -1e30


def ancestry(parents):
    node_count = parents.shape[1]
    node_ids = jnp.arange(node_count, dtype=jnp.int32)
    linked = jnp.logical_or(
        parents[:, :, None] == node_ids[None, None, :], node_ids[:, None] == node_ids[None, :]
    )
    reached = linked.astype(jnp.bfloat16)
    for doubling in range((node_count - 1).bit_length()):
        squared = jnp.einsum("aij,ajk->aik", reached, reached, preferred_element_type=jnp.float32)
        reached = jnp.minimum(squared, 1.0).astype(jnp.bfloat16)
    return reached


def body(
    queries, cache_keys, cache_values, tree_keys, tree_values, parents, tree_sizes, cache_lens
):
    group_size = NH // KVH
    softmax_scale = 1.0 / math.sqrt(HD)
    request = lax.axis_index("rh")
    quarter = lax.axis_index("rl")
    n_lo = lax.axis_size("rl")
    n_hi = lax.axis_size("rh")
    cache_block = cache_keys.shape[1]
    kv_local = cache_keys.shape[2] // HD
    heads_local = kv_local * group_size
    node_count = parents.shape[1]
    rows_owned = tree_keys.shape[0]
    by_head = lax.all_to_all(queries, "head", split_axis=1, concat_axis=0, tiled=True)
    query_block = lax.all_gather(by_head, "rl", axis=0, tiled=True)
    query_block = query_block.reshape(node_count, kv_local, group_size, HD)
    both = jnp.concatenate([cache_keys, cache_values], axis=2)
    mine = lax.all_to_all(both, "rh", split_axis=0, concat_axis=1, tiled=True)[0]
    mine = mine.reshape(n_hi, cache_block, 2, kv_local, HD)
    reached = ancestry(parents)
    ancestors = lax.dynamic_index_in_dim(reached, request, 0, keepdims=False)
    ancestors = lax.dynamic_slice_in_dim(ancestors, quarter * rows_owned, rows_owned, 1)
    live_tree_all = ancestors > 0.5
    length = lax.dynamic_index_in_dim(cache_lens, request, 0, keepdims=False)
    local_tree_keys = tree_keys.reshape(rows_owned, kv_local, HD)
    local_tree_values = tree_values.reshape(rows_owned, kv_local, HD)

    def one_group(s):
        block = s * n_lo + quarter
        positions = block * cache_block + jnp.arange(cache_block, dtype=jnp.int32)
        live_cache = positions < length
        live_tree = jnp.logical_and(live_tree_all, s == request)
        block_keys = mine[s, :, 0]
        block_values = mine[s, :, 1]
        cache_scores = (
            jnp.einsum(
                "igqd,pgd->igqp", query_block, block_keys, preferred_element_type=jnp.float32
            )
            * softmax_scale
        )
        cache_scores = jnp.where(live_cache[None, None, None, :], cache_scores, negative_fill)
        tree_scores = (
            jnp.einsum(
                "igqd,rgd->igqr", query_block, local_tree_keys, preferred_element_type=jnp.float32
            )
            * softmax_scale
        )
        tree_scores = jnp.where(live_tree[:, None, None, :], tree_scores, negative_fill)
        peaks = jnp.maximum(jnp.max(cache_scores, axis=3), jnp.max(tree_scores, axis=3))
        cache_weights = jnp.where(
            live_cache[None, None, None, :], jnp.exp(cache_scores - peaks[..., None]), 0.0
        )
        tree_weights = jnp.where(
            live_tree[:, None, None, :], jnp.exp(tree_scores - peaks[..., None]), 0.0
        )
        totals = jnp.sum(cache_weights, axis=3) + jnp.sum(tree_weights, axis=3)
        group_sums = jnp.einsum(
            "igqp,pgd->igqd",
            cache_weights.astype(jnp.bfloat16),
            block_values,
            preferred_element_type=jnp.float32,
        )
        group_sums = group_sums + jnp.einsum(
            "igqr,rgd->igqd",
            tree_weights.astype(jnp.bfloat16),
            local_tree_values,
            preferred_element_type=jnp.float32,
        )
        floored = jnp.maximum(totals, 1.0)
        partial_value = group_sums / floored[..., None]
        log_total = peaks + jnp.log(floored)
        return (
            partial_value.reshape(node_count, heads_local, HD),
            log_total.reshape(node_count, heads_local),
        )

    partials, log_totals = lax.map(one_group, jnp.arange(n_hi, dtype=jnp.int32))
    top = jnp.max(log_totals, axis=0)
    weights = jnp.exp(log_totals - top)
    den = jnp.sum(weights, axis=0)
    acc = jnp.sum(weights[..., None] * partials, axis=0)
    payload = jnp.concatenate(
        [acc.reshape(node_count, heads_local * HD), den, top], axis=1
    ).reshape(n_lo, rows_owned, heads_local * HD + 2 * heads_local)
    gathered = lax.all_to_all(payload, "rl", split_axis=0, concat_axis=0, tiled=True)
    got_acc = gathered[:, :, : heads_local * HD].reshape(n_lo, rows_owned, heads_local, HD)
    got_den = gathered[:, :, heads_local * HD : heads_local * HD + heads_local]
    got_top = gathered[:, :, heads_local * HD + heads_local :]
    highest = jnp.max(got_top, axis=0)
    scale = jnp.exp(got_top - highest)
    num = jnp.sum(scale[..., None] * got_acc, axis=0)
    total = jnp.sum(scale * got_den, axis=0)
    merged = (num / total[..., None]).reshape(rows_owned, heads_local * HD)
    row_nodes = quarter * rows_owned + jnp.arange(rows_owned, dtype=jnp.int32)
    live_size = lax.dynamic_index_in_dim(tree_sizes, request, 0, keepdims=False)
    live_rows = row_nodes < live_size
    return jnp.where(live_rows[:, None], merged, 0.0).astype(jnp.bfloat16)


def solution(mesh):

    def run(
        queries, cache_keys, cache_values, tree_keys, tree_values, parents, tree_sizes, cache_lens
    ):
        n_hi = cache_keys.shape[0]
        n_lo = mesh.shape["req"] // n_hi
        split = Mesh(mesh.devices.reshape(n_hi, n_lo, mesh.shape["head"]), ("rh", "rl", "head"))
        rows = ("rh", "rl")
        placed = (
            P(("rh", "rl", "head"), None),
            P(None, rows, "head"),
            P(None, rows, "head"),
            P(rows, "head"),
            P(rows, "head"),
            P(),
            P(),
            P(),
        )
        return jax.shard_map(
            body, mesh=split, in_specs=placed, out_specs=P(rows, "head"), check_vma=False
        )(
            queries,
            cache_keys,
            cache_values,
            tree_keys,
            tree_values,
            parents,
            tree_sizes,
            cache_lens,
        )

    return run
```

profile of v0, /device:TPU:1, one launch (start us, length us, event | category | flops | bytes accessed | tf_op | source)
XLA Modules:
  0.0 273.4 jit_solution(10835699050133776124)
XLA Ops:
  0.0 9.1 %all-to-all-start.1 = ((bf16[4,8,2048]{2,0,1:T(4,128)(2,1)}), bf16[4,8,2048]{2,0,1:T(4,128)(2,1)S(1)}, u32[]{:S(2)}, u32[]{:S(2)}) async-start(bf16[4,8,2048]{2,0,1:T(4,128)(2,1)} %bitcast.168), calls=%async_computation.1 | async-start | bytes 262144 | tf_op jit(solution)/shard_map/all_to_all | solution.py:41
  9.2 2.9 %copy.62 = bf16[8,1024,128]{1,2,0:T(8,128)(2,1)S(1)} copy(bf16[8,1024,128]{2,1,0:T(8,128)(2,1)} %param.12) | data formatting | bytes 4194304 | tf_op args[2]
  12.0 3.9 %copy.61 = bf16[8,1024,128]{1,2,0:T(8,128)(2,1)} copy(bf16[8,1024,128]{2,1,0:T(8,128)(2,1)} %param.11) | data formatting | bytes 4194304 | tf_op args[1]
  16.0 4.2 %pad_maximum_fusion = bf16[8,1024,256]{1,2,0:T(8,128)(2,1)} fusion(bf16[8,1024,128]{1,2,0:T(8,128)(2,1)S(1)} %copy.62, bf16[8,1024,128]{1,2,0:T(8,128)(2,1)} %copy.61), kind=kLoop, calls=%fused_computation.47 | loop fusion | flops 8388608 | bytes 8388608 | tf_op jit(solution)/shard_map/concatenate | solution.py:44
  20.2 6.7 %all-to-all-start = ((bf16[8,1024,256]{1,2,0:T(8,128)(2,1)}), bf16[8,1024,256]{1,2,0:T(8,128)(2,1)}, u32[]{:S(2)}, u32[]{:S(2)}) async-start(bf16[8,1024,256]{1,2,0:T(8,128)(2,1)} %pad_maximum_fusion), calls=%async_computation | async-start | bytes 8388608 | tf_op jit(solution)/shard_map/all_to_all | solution.py:45
  29.7 47.9 %all_gather.3 = bf16[128,2048]{1,0:T(8,128)(2,1)S(1)} all-gather(bf16[32,2048]{1,0:T(8,128)(2,1)S(1)} %all_to_all.28), channel_id=1, replica_groups=mesh['rh'=8,'rl'=4,'head'=8] {'rl'}, dimensions={0}, use_global_device_ids=true | all-gather | bytes 655360 | tf_op jit(solution)/shard_map/all_gather | solution.py:42
  78.5 6.5 %copy.69 = bf16[8,1024,2,1,128]{4,1,3,2,0:T(8,128)(2,1)} copy(bf16[8,1024,2,1,128]{1,4,2,0,3:T(8,128)(2,1)} %bitcast.20) | data formatting | bytes 8388608 | tf_op jit(solution)/shard_map/while | solution.py:104
  85.0 160.4 %while.14 = (s32[]{:T(128)}, f32[8,128,16,128]{1,3,2,0:T(8,128)}, f32[8,128,16]{1,2,0:T(8,128)S(1)}, s32[8]{0:T(128)S(1)}, bf16[8,1024,2,1,128]{4,1,3,2,0:T(8,12...) while((s32[]{:T(128)}, f32[8,128,16,128]{1,3,2,0:T(8,128)}, ...), condition=%wide.region_5.6_spmd, body=%wide.region_0.5_spmd.sunk | while | flops 1119164416 | bytes 55485768 | solution.py:104
  88.9 5.5 %bitcast_reduce_fusion.2 = (f32[128,16]{0,1:T(8,128)S(1)}, f32[1024,128,16]{1,0,2:T(8,128)}) fusion(pred[1024]{0:T(1024)(128)(4,1)S(1)} %add_compare_fusion.3, bf16[128,1,16,128]{3,0,2,1:T(8,128)(2,1)S(1)} %get-tuple-element.349, bf16[8,1024,2,1,128]{4,1,3,2,0:T(8,128)(2,1)} %get-tuple-element.346, s32[]{:T(128)S(6)} %select_n.118), kind=kOutput, calls=%fused_computation.1.clone.1 | convolution fusion | flops 543160320 | bytes 9184260 | tf_op jit(solution)/shard_map/while/body/eval_jaxpr/igqd,pgd->igqp/dot_general | solution.py:63
  95.2 5.8 %fusion.85 = f32[128,128,16]{1,0,2:T(8,128)S(1)} fusion(f32[1024,128,16]{1,0,2:T(8,128)} %get-tuple-element.304, f32[128,16]{0,1:T(8,128)S(1)} %max.47, pred[1024]{0:T(1024)(128)(4,1)S(1)} %add_compare_fusion.3, bf16[8,1024,2,1,128]{4,1,3,2,0:T(8,128)(2,1)} %get-tuple-element.346, s32[]{:T(128)S(6)} %select_n.118), kind=kOutput, calls=%fused_computation.8.clone.1 | convolution fusion | flops 547356672 | bytes 9709572 | tf_op jit(solution)/shard_map/while/body/eval_jaxpr/igqp,pgd->igqd/dot_general | solution.py:84
  101.0 2.5 fusion.86
  108.9 5.5 %bitcast_reduce_fusion.2 = (f32[128,16]{0,1:T(8,128)S(1)}, f32[1024,128,16]{1,0,2:T(8,128)}) fusion(pred[1024]{0:T(1024)(128)(4,1)S(1)} %add_compare_fusion.3, bf16[128,1,16,128]{3,0,2,1:T(8,128)(2,1)S(1)} %get-tuple-element.349, bf16[8,1024,2,1,128]{4,1,3,2,0:T(8,128)(2,1)} %get-tuple-element.346, s32[]{:T(128)S(6)} %select_n.118), kind=kOutput, calls=%fused_computation.1.clone.1 | convolution fusion | flops 543160320 | bytes 9184260 | tf_op jit(solution)/shard_map/while/body/eval_jaxpr/igqd,pgd->igqp/dot_general | solution.py:63
  115.2 5.8 %fusion.85 = f32[128,128,16]{1,0,2:T(8,128)S(1)} fusion(f32[1024,128,16]{1,0,2:T(8,128)} %get-tuple-element.304, f32[128,16]{0,1:T(8,128)S(1)} %max.47, pred[1024]{0:T(1024)(128)(4,1)S(1)} %add_compare_fusion.3, bf16[8,1024,2,1,128]{4,1,3,2,0:T(8,128)(2,1)} %get-tuple-element.346, s32[]{:T(128)S(6)} %select_n.118), kind=kOutput, calls=%fused_computation.8.clone.1 | convolution fusion | flops 547356672 | bytes 9709572 | tf_op jit(solution)/shard_map/while/body/eval_jaxpr/igqp,pgd->igqd/dot_general | solution.py:84
  121.1 2.5 fusion.86
  129.0 5.5 %bitcast_reduce_fusion.2 = (f32[128,16]{0,1:T(8,128)S(1)}, f32[1024,128,16]{1,0,2:T(8,128)}) fusion(pred[1024]{0:T(1024)(128)(4,1)S(1)} %add_compare_fusion.3, bf16[128,1,16,128]{3,0,2,1:T(8,128)(2,1)S(1)} %get-tuple-element.349, bf16[8,1024,2,1,128]{4,1,3,2,0:T(8,128)(2,1)} %get-tuple-element.346, s32[]{:T(128)S(6)} %select_n.118), kind=kOutput, calls=%fused_computation.1.clone.1 | convolution fusion | flops 543160320 | bytes 9184260 | tf_op jit(solution)/shard_map/while/body/eval_jaxpr/igqd,pgd->igqp/dot_general | solution.py:63
  135.3 5.8 %fusion.85 = f32[128,128,16]{1,0,2:T(8,128)S(1)} fusion(f32[1024,128,16]{1,0,2:T(8,128)} %get-tuple-element.304, f32[128,16]{0,1:T(8,128)S(1)} %max.47, pred[1024]{0:T(1024)(128)(4,1)S(1)} %add_compare_fusion.3, bf16[8,1024,2,1,128]{4,1,3,2,0:T(8,128)(2,1)} %get-tuple-element.346, s32[]{:T(128)S(6)} %select_n.118), kind=kOutput, calls=%fused_computation.8.clone.1 | convolution fusion | flops 547356672 | bytes 9709572 | tf_op jit(solution)/shard_map/while/body/eval_jaxpr/igqp,pgd->igqd/dot_general | solution.py:84
  141.2 2.5 fusion.86
  149.1 5.5 %bitcast_reduce_fusion.2 = (f32[128,16]{0,1:T(8,128)S(1)}, f32[1024,128,16]{1,0,2:T(8,128)}) fusion(pred[1024]{0:T(1024)(128)(4,1)S(1)} %add_compare_fusion.3, bf16[128,1,16,128]{3,0,2,1:T(8,128)(2,1)S(1)} %get-tuple-element.349, bf16[8,1024,2,1,128]{4,1,3,2,0:T(8,128)(2,1)} %get-tuple-element.346, s32[]{:T(128)S(6)} %select_n.118), kind=kOutput, calls=%fused_computation.1.clone.1 | convolution fusion | flops 543160320 | bytes 9184260 | tf_op jit(solution)/shard_map/while/body/eval_jaxpr/igqd,pgd->igqp/dot_general | solution.py:63
  155.3 5.8 %fusion.85 = f32[128,128,16]{1,0,2:T(8,128)S(1)} fusion(f32[1024,128,16]{1,0,2:T(8,128)} %get-tuple-element.304, f32[128,16]{0,1:T(8,128)S(1)} %max.47, pred[1024]{0:T(1024)(128)(4,1)S(1)} %add_compare_fusion.3, bf16[8,1024,2,1,128]{4,1,3,2,0:T(8,128)(2,1)} %get-tuple-element.346, s32[]{:T(128)S(6)} %select_n.118), kind=kOutput, calls=%fused_computation.8.clone.1 | convolution fusion | flops 547356672 | bytes 9709572 | tf_op jit(solution)/shard_map/while/body/eval_jaxpr/igqp,pgd->igqd/dot_general | solution.py:84
  161.2 2.5 fusion.86
  169.1 5.5 %bitcast_reduce_fusion.2 = (f32[128,16]{0,1:T(8,128)S(1)}, f32[1024,128,16]{1,0,2:T(8,128)}) fusion(pred[1024]{0:T(1024)(128)(4,1)S(1)} %add_compare_fusion.3, bf16[128,1,16,128]{3,0,2,1:T(8,128)(2,1)S(1)} %get-tuple-element.349, bf16[8,1024,2,1,128]{4,1,3,2,0:T(8,128)(2,1)} %get-tuple-element.346, s32[]{:T(128)S(6)} %select_n.118), kind=kOutput, calls=%fused_computation.1.clone.1 | convolution fusion | flops 543160320 | bytes 9184260 | tf_op jit(solution)/shard_map/while/body/eval_jaxpr/igqd,pgd->igqp/dot_general | solution.py:63
  175.4 5.8 %fusion.85 = f32[128,128,16]{1,0,2:T(8,128)S(1)} fusion(f32[1024,128,16]{1,0,2:T(8,128)} %get-tuple-element.304, f32[128,16]{0,1:T(8,128)S(1)} %max.47, pred[1024]{0:T(1024)(128)(4,1)S(1)} %add_compare_fusion.3, bf16[8,1024,2,1,128]{4,1,3,2,0:T(8,128)(2,1)} %get-tuple-element.346, s32[]{:T(128)S(6)} %select_n.118), kind=kOutput, calls=%fused_computation.8.clone.1 | convolution fusion | flops 547356672 | bytes 9709572 | tf_op jit(solution)/shard_map/while/body/eval_jaxpr/igqp,pgd->igqd/dot_general | solution.py:84
  181.2 2.5 fusion.86
  189.1 5.5 %bitcast_reduce_fusion.2 = (f32[128,16]{0,1:T(8,128)S(1)}, f32[1024,128,16]{1,0,2:T(8,128)}) fusion(pred[1024]{0:T(1024)(128)(4,1)S(1)} %add_compare_fusion.3, bf16[128,1,16,128]{3,0,2,1:T(8,128)(2,1)S(1)} %get-tuple-element.349, bf16[8,1024,2,1,128]{4,1,3,2,0:T(8,128)(2,1)} %get-tuple-element.346, s32[]{:T(128)S(6)} %select_n.118), kind=kOutput, calls=%fused_computation.1.clone.1 | convolution fusion | flops 543160320 | bytes 9184260 | tf_op jit(solution)/shard_map/while/body/eval_jaxpr/igqd,pgd->igqp/dot_general | solution.py:63
  195.4 5.8 %fusion.85 = f32[128,128,16]{1,0,2:T(8,128)S(1)} fusion(f32[1024,128,16]{1,0,2:T(8,128)} %get-tuple-element.304, f32[128,16]{0,1:T(8,128)S(1)} %max.47, pred[1024]{0:T(1024)(128)(4,1)S(1)} %add_compare_fusion.3, bf16[8,1024,2,1,128]{4,1,3,2,0:T(8,128)(2,1)} %get-tuple-element.346, s32[]{:T(128)S(6)} %select_n.118), kind=kOutput, calls=%fused_computation.8.clone.1 | convolution fusion | flops 547356672 | bytes 9709572 | tf_op jit(solution)/shard_map/while/body/eval_jaxpr/igqp,pgd->igqd/dot_general | solution.py:84
  209.2 5.5 %bitcast_reduce_fusion.2 = (f32[128,16]{0,1:T(8,128)S(1)}, f32[1024,128,16]{1,0,2:T(8,128)}) fusion(pred[1024]{0:T(1024)(128)(4,1)S(1)} %add_compare_fusion.3, bf16[128,1,16,128]{3,0,2,1:T(8,128)(2,1)S(1)} %get-tuple-element.349, bf16[8,1024,2,1,128]{4,1,3,2,0:T(8,128)(2,1)} %get-tuple-element.346, s32[]{:T(128)S(6)} %select_n.118), kind=kOutput, calls=%fused_computation.1.clone.1 | convolution fusion | flops 543160320 | bytes 9184260 | tf_op jit(solution)/shard_map/while/body/eval_jaxpr/igqd,pgd->igqp/dot_general | solution.py:63
  215.5 5.8 %fusion.85 = f32[128,128,16]{1,0,2:T(8,128)S(1)} fusion(f32[1024,128,16]{1,0,2:T(8,128)} %get-tuple-element.304, f32[128,16]{0,1:T(8,128)S(1)} %max.47, pred[1024]{0:T(1024)(128)(4,1)S(1)} %add_compare_fusion.3, bf16[8,1024,2,1,128]{4,1,3,2,0:T(8,128)(2,1)} %get-tuple-element.346, s32[]{:T(128)S(6)} %select_n.118), kind=kOutput, calls=%fused_computation.8.clone.1 | convolution fusion | flops 547356672 | bytes 9709572 | tf_op jit(solution)/shard_map/while/body/eval_jaxpr/igqp,pgd->igqd/dot_general | solution.py:84
  229.3 5.5 %bitcast_reduce_fusion.2 = (f32[128,16]{0,1:T(8,128)S(1)}, f32[1024,128,16]{1,0,2:T(8,128)}) fusion(pred[1024]{0:T(1024)(128)(4,1)S(1)} %add_compare_fusion.3, bf16[128,1,16,128]{3,0,2,1:T(8,128)(2,1)S(1)} %get-tuple-element.349, bf16[8,1024,2,1,128]{4,1,3,2,0:T(8,128)(2,1)} %get-tuple-element.346, s32[]{:T(128)S(6)} %select_n.118), kind=kOutput, calls=%fused_computation.1.clone.1 | convolution fusion | flops 543160320 | bytes 9184260 | tf_op jit(solution)/shard_map/while/body/eval_jaxpr/igqd,pgd->igqp/dot_general | solution.py:63
  235.5 5.8 %fusion.85 = f32[128,128,16]{1,0,2:T(8,128)S(1)} fusion(f32[1024,128,16]{1,0,2:T(8,128)} %get-tuple-element.304, f32[128,16]{0,1:T(8,128)S(1)} %max.47, pred[1024]{0:T(1024)(128)(4,1)S(1)} %add_compare_fusion.3, bf16[8,1024,2,1,128]{4,1,3,2,0:T(8,128)(2,1)} %get-tuple-element.346, s32[]{:T(128)S(6)} %select_n.118), kind=kOutput, calls=%fused_computation.8.clone.1 | convolution fusion | flops 547356672 | bytes 9709572 | tf_op jit(solution)/shard_map/while/body/eval_jaxpr/igqp,pgd->igqd/dot_general | solution.py:84
  245.5 4.8 %multiply_reduce_fusion = f32[128,16,128]{0,2,1:T(8,128)S(1)} fusion(f32[8,128,16,128]{1,3,2,0:T(8,128)} %get-tuple-element.146, f32[8,128,16]{1,2,0:T(8,128)S(1)} %get-tuple-element.224), kind=kLoop, calls=%fused_computation.46 | loop fusion | flops 3932160 | bytes 9502720 | tf_op jit(solution)/shard_map/reduce_sum | solution.py:108
  252.2 5.2 %all-to-all-start.2 = ((f32[4,32,2080]{2,1,0:T(8,128)}), f32[4,32,2080]{2,1,0:T(8,128)S(1)}, u32[]{:S(2)}, u32[]{:S(2)}) async-start(f32[4,32,2080]{2,1,0:T(8,128)} %concatenate.17), calls=%async_computation.2 | async-start | bytes 2228224 | tf_op jit(solution)/shard_map/all_to_all | solution.py:112
  258.7 13.1 %all-to-all-done.2 = f32[4,32,2080]{2,1,0:T(8,128)S(1)} async-done(((f32[4,32,2080]{2,1,0:T(8,128)}), f32[4,32,2080]{2,1,0:T(8,128)S(1)}, u32[]{:S(2)}, u32[]{:S(2)}) %all-to-all-start.2) | async-done | bytes 1064992 | tf_op jit(solution)/shard_map/all_to_all | solution.py:112
  (150 shorter events, 38.4 us)
Async XLA Ops:
  0.0 78.3 %copy-start = (bf16[32,128]{1,0:T(8,128)(2,1)S(1)}, bf16[32,128]{1,0:T(8,128)(2,1)}, u32[]{:S(2)}) copy-start(bf16[32,128]{1,0:T(8,128)(2,1)} %param.13) | copy-start | bytes 24580
  0.0 20.2 %all-to-all-start.1 = ((bf16[4,8,2048]{2,0,1:T(4,128)(2,1)}), bf16[4,8,2048]{2,0,1:T(4,128)(2,1)S(1)}, u32[]{:S(2)}, u32[]{:S(2)}) async-start(bf16[4,8,2048]{2,0,1:T(4,128)(2,1)} %bitcast.168), calls=%async_computation.1 | async-start | bytes 262144 | tf_op jit(solution)/shard_map/all_to_all | solution.py:41
  16.0 10.9 %copy-start.3 = (s32[8]{0:T(128)S(1)}, s32[8]{0:T(128)}, u32[]{:S(2)}) copy-start(s32[8]{0:T(128)} %param.17) | copy-start | bytes 100
  16.0 11.5 %copy-start.2 = (s32[8,128]{1,0:T(8,128)S(1)}, s32[8,128]{1,0:T(8,128)}, u32[]{:S(2)}) copy-start(s32[8,128]{1,0:T(8,128)} %param.15) | copy-start | bytes 12292
  20.2 58.3 %all-to-all-start = ((bf16[8,1024,256]{1,2,0:T(8,128)(2,1)}), bf16[8,1024,256]{1,2,0:T(8,128)(2,1)}, u32[]{:S(2)}, u32[]{:S(2)}) async-start(bf16[8,1024,256]{1,2,0:T(8,128)(2,1)} %pad_maximum_fusion), calls=%async_computation | async-start | bytes 8388608 | tf_op jit(solution)/shard_map/all_to_all | solution.py:45
  26.8 58.1 %copy-start.1 = (bf16[32,128]{1,0:T(8,128)(2,1)S(1)}, bf16[32,128]{1,0:T(8,128)(2,1)}, u32[]{:S(2)}) copy-start(bf16[32,128]{1,0:T(8,128)(2,1)} %param.14) | copy-start | bytes 24580
  95.1 5.9 %slice-start = ((s8[8388608]{0:T(1024)(128)(4,1)}), s8[4194304]{0:T(1024)(128)(4,1)S(1)}, s32[]{:S(2)}) async-start(s8[8388608]{0:T(1024)(128)(4,1)} %bitcast.160), calls=%async_computation.3 | async-start | bytes 8388608 | tf_op jit(solution)/shard_map/while
  95.2 5.9 %slice-start.1 = ((s8[8388608]{0:T(1024)(128)(4,1)}), s8[4194304]{0:T(1024)(128)(4,1)S(1)}, s32[]{:S(2)}) async-start(s8[8388608]{0:T(1024)(128)(4,1)} %bitcast.160), calls=%async_computation.4 | async-start | bytes 8388608 | tf_op jit(solution)/shard_map/while
  115.1 5.9 %slice-start = ((s8[8388608]{0:T(1024)(128)(4,1)}), s8[4194304]{0:T(1024)(128)(4,1)S(1)}, s32[]{:S(2)}) async-start(s8[8388608]{0:T(1024)(128)(4,1)} %bitcast.160), calls=%async_computation.3 | async-start | bytes 8388608 | tf_op jit(solution)/shard_map/while
  115.2 5.9 %slice-start.1 = ((s8[8388608]{0:T(1024)(128)(4,1)}), s8[4194304]{0:T(1024)(128)(4,1)S(1)}, s32[]{:S(2)}) async-start(s8[8388608]{0:T(1024)(128)(4,1)} %bitcast.160), calls=%async_computation.4 | async-start | bytes 8388608 | tf_op jit(solution)/shard_map/while
  135.2 5.9 %slice-start = ((s8[8388608]{0:T(1024)(128)(4,1)}), s8[4194304]{0:T(1024)(128)(4,1)S(1)}, s32[]{:S(2)}) async-start(s8[8388608]{0:T(1024)(128)(4,1)} %bitcast.160), calls=%async_computation.3 | async-start | bytes 8388608 | tf_op jit(solution)/shard_map/while
  135.3 5.9 %slice-start.1 = ((s8[8388608]{0:T(1024)(128)(4,1)}), s8[4194304]{0:T(1024)(128)(4,1)S(1)}, s32[]{:S(2)}) async-start(s8[8388608]{0:T(1024)(128)(4,1)} %bitcast.160), calls=%async_computation.4 | async-start | bytes 8388608 | tf_op jit(solution)/shard_map/while
  155.2 5.9 %slice-start = ((s8[8388608]{0:T(1024)(128)(4,1)}), s8[4194304]{0:T(1024)(128)(4,1)S(1)}, s32[]{:S(2)}) async-start(s8[8388608]{0:T(1024)(128)(4,1)} %bitcast.160), calls=%async_computation.3 | async-start | bytes 8388608 | tf_op jit(solution)/shard_map/while
  155.3 5.9 %slice-start.1 = ((s8[8388608]{0:T(1024)(128)(4,1)}), s8[4194304]{0:T(1024)(128)(4,1)S(1)}, s32[]{:S(2)}) async-start(s8[8388608]{0:T(1024)(128)(4,1)} %bitcast.160), calls=%async_computation.4 | async-start | bytes 8388608 | tf_op jit(solution)/shard_map/while
  175.3 5.9 %slice-start = ((s8[8388608]{0:T(1024)(128)(4,1)}), s8[4194304]{0:T(1024)(128)(4,1)S(1)}, s32[]{:S(2)}) async-start(s8[8388608]{0:T(1024)(128)(4,1)} %bitcast.160), calls=%async_computation.3 | async-start | bytes 8388608 | tf_op jit(solution)/shard_map/while
  175.4 5.9 %slice-start.1 = ((s8[8388608]{0:T(1024)(128)(4,1)}), s8[4194304]{0:T(1024)(128)(4,1)S(1)}, s32[]{:S(2)}) async-start(s8[8388608]{0:T(1024)(128)(4,1)} %bitcast.160), calls=%async_computation.4 | async-start | bytes 8388608 | tf_op jit(solution)/shard_map/while
  195.3 5.9 %slice-start = ((s8[8388608]{0:T(1024)(128)(4,1)}), s8[4194304]{0:T(1024)(128)(4,1)S(1)}, s32[]{:S(2)}) async-start(s8[8388608]{0:T(1024)(128)(4,1)} %bitcast.160), calls=%async_computation.3 | async-start | bytes 8388608 | tf_op jit(solution)/shard_map/while
  195.4 5.9 %slice-start.1 = ((s8[8388608]{0:T(1024)(128)(4,1)}), s8[4194304]{0:T(1024)(128)(4,1)S(1)}, s32[]{:S(2)}) async-start(s8[8388608]{0:T(1024)(128)(4,1)} %bitcast.160), calls=%async_computation.4 | async-start | bytes 8388608 | tf_op jit(solution)/shard_map/while
  215.4 5.9 %slice-start = ((s8[8388608]{0:T(1024)(128)(4,1)}), s8[4194304]{0:T(1024)(128)(4,1)S(1)}, s32[]{:S(2)}) async-start(s8[8388608]{0:T(1024)(128)(4,1)} %bitcast.160), calls=%async_computation.3 | async-start | bytes 8388608 | tf_op jit(solution)/shard_map/while
  215.5 5.9 %slice-start.1 = ((s8[8388608]{0:T(1024)(128)(4,1)}), s8[4194304]{0:T(1024)(128)(4,1)S(1)}, s32[]{:S(2)}) async-start(s8[8388608]{0:T(1024)(128)(4,1)} %bitcast.160), calls=%async_computation.4 | async-start | bytes 8388608 | tf_op jit(solution)/shard_map/while
  235.4 5.9 %slice-start = ((s8[8388608]{0:T(1024)(128)(4,1)}), s8[4194304]{0:T(1024)(128)(4,1)S(1)}, s32[]{:S(2)}) async-start(s8[8388608]{0:T(1024)(128)(4,1)} %bitcast.160), calls=%async_computation.3 | async-start | bytes 8388608 | tf_op jit(solution)/shard_map/while
  235.5 5.9 %slice-start.1 = ((s8[8388608]{0:T(1024)(128)(4,1)}), s8[4194304]{0:T(1024)(128)(4,1)S(1)}, s32[]{:S(2)}) async-start(s8[8388608]{0:T(1024)(128)(4,1)} %bitcast.160), calls=%async_computation.4 | async-start | bytes 8388608 | tf_op jit(solution)/shard_map/while
  245.5 11.9 %copy-start.4 = (s32[8]{0:T(128)S(1)}, s32[8]{0:T(128)}, u32[]{:S(2)}) copy-start(s32[8]{0:T(128)} %param.16) | copy-start | bytes 100
  252.2 19.5 %all-to-all-start.2 = ((f32[4,32,2080]{2,1,0:T(8,128)}), f32[4,32,2080]{2,1,0:T(8,128)S(1)}, u32[]{:S(2)}, u32[]{:S(2)}) async-start(f32[4,32,2080]{2,1,0:T(8,128)} %concatenate.17), calls=%async_computation.2 | async-start | bytes 2228224 | tf_op jit(solution)/shard_map/all_to_all | solution.py:112
where the time goes:
time: 275 us; the launch traced here: 273 us
  matrix products  103 us (37%)
  blocking collectives  47.9 us (17%)
  other arithmetic  36.8 us (13%)
  loops' own time  27.8 us (10%)
  local copies, waits for them, and re-layouts  23.5 us (9%)
  starting transfers between devices  21 us (8%)
  waiting for transfers between devices  13.1 us (5%)
    all_gather x1, blocking collectives, body(): query_block = lax.all_gather(by_head, 'rl', axis=0, tiled=True)  47.9 us
    dot_general x8, matrix products, one_group(): jnp.einsum('igqp,pgd->igqd', cache_weights.astype(jnp.bfloat16), block_va...  46.3 us
    dot_general x8, matrix products, one_group(): jnp.einsum('igqd,pgd->igqp', query_block, block_keys, preferred_element_t...  43.9 us
    another operation x1, loops' own time, body(): partials, log_totals = lax.map(one_group, jnp.arange(n_hi, dtype=jnp.int32))  27.8 us
    reduce_sum x16, other arithmetic, one_group(): totals = jnp.sum(cache_weights, axis=3) + jnp.sum(tree_weights, axis=3)  20.8 us
    all_to_all x1, waiting for transfers between devices, body(): lax.all_to_all(payload, 'rl', split_axis=0, concat_axis=0, tiled=True)  13.1 us
    dot_general x8, matrix products, one_group(): jnp.einsum('igqr,rgd->igqd', tree_weights.astype(jnp.bfloat16), local_tre...  10.8 us
    all_to_all x1, starting transfers between devices, body(): lax.all_to_all(queries, 'head', split_axis=1, concat_axis=0, tiled=True)  9.15 us
  transfers between devices with their start and end apart: 3, of which 1 were waited for; matrix products, arithmetic and copies ran while one was open for 6% of the time, Pallas kernels for 0%

commit v1 on v0

--- a/solution.py
+++ b/solution.py
@@ -9,6 +9,17 @@
 KVH = 8
 HD = 128
 negative_fill = -1e30
+
+
+def split_up(x, dim, size):
+    before, after = (x.shape[:dim], x.shape[dim + 1 :])
+    return jnp.moveaxis(x.reshape(*before, size, -1, *after), dim, 0)
+
+
+def laid_out(blocks, dim):
+    blocks = jnp.moveaxis(blocks, 0, dim)
+    dims = blocks.shape
+    return blocks.reshape(*dims[:dim], dims[dim] * dims[dim + 1], *dims[dim + 2 :])
 
 
 def ancestry(parents):
@@ -38,7 +49,14 @@
     heads_local = kv_local * group_size
     node_count = parents.shape[1]
     rows_owned = tree_keys.shape[0]
-    by_head = lax.all_to_all(queries, "head", split_axis=1, concat_axis=0, tiled=True)
+    count, position = (lax.axis_size("head"), lax.axis_index("head"))
+    tiles = split_up(queries, 1, count)
+    finished = [tiles[position]]
+    for turn in range(1, count):
+        sent = tiles[position ^ turn]
+        finished.append(lax.ppermute(sent, "head", [(i, i ^ turn) for i in range(count)]))
+    tiles = jnp.stack(finished)[position ^ jnp.arange(count)]
+    by_head = laid_out(tiles, 0)
     query_block = lax.all_gather(by_head, "rl", axis=0, tiled=True)
     query_block = query_block.reshape(node_count, kv_local, group_size, HD)
     both = jnp.concatenate([cache_keys, cache_values], axis=2)

time: 275 us -> 266 us (0.967)
  blocking collectives: 47.9 us -> 28.1 us
  starting transfers between devices: 21 us -> 27.4 us
  waiting for transfers between devices: 13.1 us -> 17.1 us
    all_gather x1, blocking collectives: 47.9 us -> 28.1 us  [body(): query_block = lax.all_gather(by_head, 'rl', axis=0, tiled=True)]
    ppermute x0 -> x7, starting transfers between devices: none -> 14.8 us  [body(): lax.ppermute(sent, 'head', [(i, i ^ turn) for i in range(count)])]
    all_to_all x1 -> x0, starting transfers between devices: 9.15 us -> none  [body(): lax.all_to_all(queries, 'head', split_axis=1, concat_axis=0, tiled=True)]
    ppermute x0 -> x7, waiting for transfers between devices: none -> 4.07 us  [body(): lax.ppermute(sent, 'head', [(i, i ^ turn) for i in range(count)])]
    unnamed x12 -> x21, local copies, waits for them, and re-layouts: 6.81 us -> 6.93 us
  transfers between devices with their start and end apart: 3 -> 9, of which waited for: 1 -> 3; matrix products, arithmetic and copies ran while one was open for 6% -> 2% of each run, Pallas kernels for 0% -> 0%
where the time goes in v1:
time: 266 us; the launch traced here: 265 us
  matrix products  103 us (39%)
  other arithmetic  36.8 us (14%)
  blocking collectives  28.1 us (11%)
  loops' own time  27.8 us (10%)
  starting transfers between devices  27.4 us (10%)
  local copies, waits for them, and re-layouts  24.3 us (9%)
  waiting for transfers between devices  17.1 us (6%)
    dot_general x8, matrix products, one_group(): jnp.einsum('igqp,pgd->igqd', cache_weights.astype(jnp.bfloat16), block_va...  46.3 us
    dot_general x8, matrix products, one_group(): jnp.einsum('igqd,pgd->igqp', query_block, block_keys, preferred_element_t...  43.8 us
    all_gather x1, blocking collectives, body(): query_block = lax.all_gather(by_head, 'rl', axis=0, tiled=True)  28.1 us
    another operation x1, loops' own time, body(): partials, log_totals = lax.map(one_group, jnp.arange(n_hi, dtype=jnp.int32))  27.8 us
    reduce_sum x16, other arithmetic, one_group(): totals = jnp.sum(cache_weights, axis=3) + jnp.sum(tree_weights, axis=3)  20.8 us
    ppermute x7, starting transfers between devices, body(): lax.ppermute(sent, 'head', [(i, i ^ turn) for i in range(count)])  14.8 us
    all_to_all x1, waiting for transfers between devices, body(): lax.all_to_all(payload, 'rl', split_axis=0, concat_axis=0, tiled=True)  13.1 us
    dot_general x8, matrix products, one_group(): jnp.einsum('igqr,rgd->igqd', tree_weights.astype(jnp.bfloat16), local_tre...  10.8 us
  transfers between devices with their start and end apart: 9, of which 3 were waited for; matrix products, arithmetic and copies ran while one was open for 2% of the time, Pallas kernels for 0%

profile of v1, /device:TPU:1, one launch (start us, length us, event | category | flops | bytes accessed | tf_op | source)
XLA Modules:
  0.0 265.1 jit_solution(8268169738429491089)
XLA Ops:
  0.0 2.9 %copy.82 = bf16[8,1024,128]{1,2,0:T(8,128)(2,1)S(1)} copy(bf16[8,1024,128]{2,1,0:T(8,128)(2,1)} %param.12) | data formatting | bytes 4194304 | tf_op args[2]
  2.9 3.9 %copy.81 = bf16[8,1024,128]{1,2,0:T(8,128)(2,1)} copy(bf16[8,1024,128]{2,1,0:T(8,128)(2,1)} %param.11) | data formatting | bytes 4194304 | tf_op args[1]
  6.8 4.2 %pad_maximum_fusion = bf16[8,1024,256]{1,2,0:T(8,128)(2,1)} fusion(bf16[8,1024,128]{1,2,0:T(8,128)(2,1)S(1)} %copy.82, bf16[8,1024,128]{1,2,0:T(8,128)(2,1)} %copy.81), kind=kLoop, calls=%fused_computation.48 | loop fusion | flops 8388608 | bytes 8388608 | tf_op jit(solution)/shard_map/concatenate | solution.py:62
  11.0 7.5 %all-to-all-start = ((bf16[8,1024,256]{1,2,0:T(8,128)(2,1)}), bf16[8,1024,256]{1,2,0:T(8,128)(2,1)}, u32[]{:S(2)}, u32[]{:S(2)}) async-start(bf16[8,1024,256]{1,2,0:T(8,128)(2,1)} %pad_maximum_fusion), calls=%async_computation | async-start | bytes 8388608 | tf_op jit(solution)/shard_map/all_to_all | solution.py:63
  20.4 3.0 %collective-permute-start.1 = (bf16[4,2048]{1,0:T(4,128)(2,1)S(1)}, bf16[4,2048]{1,0:T(4,128)(2,1)S(1)}, u32[]{:S(2)}, u32[]{:S(2)}) collective-permute-start(bf16[4,2048]{1,0:T(4,128)(2,1)S(1)} %get-tuple-element.232), channel_id=1, source_target_pairs={{0,2},{1,3},{2,0},{3,1},{4,6},{5,7},{6,4},{7,5},{8,10},{9,11},{10,... | collective-permute-start | bytes 49160 | tf_op jit(solution)/shard_map/ppermute | solution.py:57
  23.4 5.8 %collective-permute-start.3 = (bf16[4,2048]{1,0:T(4,128)(2,1)S(1)}, bf16[4,2048]{1,0:T(4,128)(2,1)S(1)}, u32[]{:S(2)}, u32[]{:S(2)}) collective-permute-start(bf16[4,2048]{1,0:T(4,128)(2,1)S(1)} %get-tuple-element.230), channel_id=1, source_target_pairs={{0,4},{1,5},{2,6},{3,7},{4,0},{5,1},{6,2},{7,3},{8,12},{9,13},{10,... | collective-permute-start | bytes 49160 | tf_op jit(solution)/shard_map/ppermute | solution.py:57
  32.1 4.1 %collective-permute-start.5 = (bf16[4,2048]{1,0:T(4,128)(2,1)S(1)}, bf16[4,2048]{1,0:T(4,128)(2,1)S(1)}, u32[]{:S(2)}, u32[]{:S(2)}) collective-permute-start(bf16[4,2048]{1,0:T(4,128)(2,1)S(1)} %get-tuple-element.228), channel_id=1, source_target_pairs={{0,6},{1,7},{2,4},{3,5},{4,2},{5,3},{6,0},{7,1},{8,14},{9,15},{10,... | collective-permute-start | bytes 49160 | tf_op jit(solution)/shard_map/ppermute | solution.py:57
  37.9 2.6 collective-permute-done.6
  41.3 28.1 %all_gather.3 = bf16[128,2048]{1,0:T(8,128)(2,1)S(1)} all-gather(bf16[32,2048]{1,0:T(8,128)(2,1)S(1)} %reshape.258), channel_id=1, replica_groups=mesh['rh'=8,'rl'=4,'head'=8] {'rl'}, dimensions={0}, use_global_device_ids=true | all-gather | bytes 655360 | tf_op jit(solution)/shard_map/all_gather | solution.py:60
  70.2 6.5 %copy.96 = bf16[8,1024,2,1,128]{4,1,3,2,0:T(8,128)(2,1)} copy(bf16[8,1024,2,1,128]{1,4,2,0,3:T(8,128)(2,1)} %bitcast.20) | data formatting | bytes 8388608 | tf_op jit(solution)/shard_map/while | solution.py:122
  76.7 160.4 %while.14 = (s32[]{:T(128)}, f32[8,128,16,128]{1,3,2,0:T(8,128)}, f32[8,128,16]{1,2,0:T(8,128)S(1)}, s32[8]{0:T(128)S(1)}, bf16[8,1024,2,1,128]{4,1,3,2,0:T(8,12...) while((s32[]{:T(128)}, f32[8,128,16,128]{1,3,2,0:T(8,128)}, ...), condition=%wide.region_5.6_spmd, body=%wide.region_0.5_spmd.sunk | while | flops 1119164416 | bytes 55485768 | solution.py:122
  80.6 5.5 %bitcast_reduce_fusion.2 = (f32[128,16]{0,1:T(8,128)S(1)}, f32[1024,128,16]{1,0,2:T(8,128)}) fusion(pred[1024]{0:T(1024)(128)(4,1)S(1)} %add_compare_fusion.3, bf16[128,1,16,128]{3,0,2,1:T(8,128)(2,1)S(1)} %get-tuple-element.356, bf16[8,1024,2,1,128]{4,1,3,2,0:T(8,128)(2,1)} %get-tuple-element.353, s32[]{:T(128)S(6)} %select_n.164), kind=kOutput, calls=%fused_computation.2.clone.1 | convolution fusion | flops 543160320 | bytes 9184260 | tf_op jit(solution)/shard_map/while/body/eval_jaxpr/igqd,pgd->igqp/dot_general | solution.py:81
  86.9 5.8 %fusion.85 = f32[128,128,16]{1,0,2:T(8,128)S(1)} fusion(f32[1024,128,16]{1,0,2:T(8,128)} %get-tuple-element.311, f32[128,16]{0,1:T(8,128)S(1)} %max.47, pred[1024]{0:T(1024)(128)(4,1)S(1)} %add_compare_fusion.3, bf16[8,1024,2,1,128]{4,1,3,2,0:T(8,128)(2,1)} %get-tuple-element.353, s32[]{:T(128)S(6)} %select_n.164), kind=kOutput, calls=%fused_computation.9.clone.1 | convolution fusion | flops 547356672 | bytes 9709572 | tf_op jit(solution)/shard_map/while/body/eval_jaxpr/igqp,pgd->igqd/dot_general | solution.py:102
  92.7 2.5 fusion.86
  100.6 5.5 %bitcast_reduce_fusion.2 = (f32[128,16]{0,1:T(8,128)S(1)}, f32[1024,128,16]{1,0,2:T(8,128)}) fusion(pred[1024]{0:T(1024)(128)(4,1)S(1)} %add_compare_fusion.3, bf16[128,1,16,128]{3,0,2,1:T(8,128)(2,1)S(1)} %get-tuple-element.356, bf16[8,1024,2,1,128]{4,1,3,2,0:T(8,128)(2,1)} %get-tuple-element.353, s32[]{:T(128)S(6)} %select_n.164), kind=kOutput, calls=%fused_computation.2.clone.1 | convolution fusion | flops 543160320 | bytes 9184260 | tf_op jit(solution)/shard_map/while/body/eval_jaxpr/igqd,pgd->igqp/dot_general | solution.py:81
  106.9 5.8 %fusion.85 = f32[128,128,16]{1,0,2:T(8,128)S(1)} fusion(f32[1024,128,16]{1,0,2:T(8,128)} %get-tuple-element.311, f32[128,16]{0,1:T(8,128)S(1)} %max.47, pred[1024]{0:T(1024)(128)(4,1)S(1)} %add_compare_fusion.3, bf16[8,1024,2,1,128]{4,1,3,2,0:T(8,128)(2,1)} %get-tuple-element.353, s32[]{:T(128)S(6)} %select_n.164), kind=kOutput, calls=%fused_computation.9.clone.1 | convolution fusion | flops 547356672 | bytes 9709572 | tf_op jit(solution)/shard_map/while/body/eval_jaxpr/igqp,pgd->igqd/dot_general | solution.py:102
  112.8 2.5 fusion.86
  120.7 5.5 %bitcast_reduce_fusion.2 = (f32[128,16]{0,1:T(8,128)S(1)}, f32[1024,128,16]{1,0,2:T(8,128)}) fusion(pred[1024]{0:T(1024)(128)(4,1)S(1)} %add_compare_fusion.3, bf16[128,1,16,128]{3,0,2,1:T(8,128)(2,1)S(1)} %get-tuple-element.356, bf16[8,1024,2,1,128]{4,1,3,2,0:T(8,128)(2,1)} %get-tuple-element.353, s32[]{:T(128)S(6)} %select_n.164), kind=kOutput, calls=%fused_computation.2.clone.1 | convolution fusion | flops 543160320 | bytes 9184260 | tf_op jit(solution)/shard_map/while/body/eval_jaxpr/igqd,pgd->igqp/dot_general | solution.py:81
  127.0 5.8 %fusion.85 = f32[128,128,16]{1,0,2:T(8,128)S(1)} fusion(f32[1024,128,16]{1,0,2:T(8,128)} %get-tuple-element.311, f32[128,16]{0,1:T(8,128)S(1)} %max.47, pred[1024]{0:T(1024)(128)(4,1)S(1)} %add_compare_fusion.3, bf16[8,1024,2,1,128]{4,1,3,2,0:T(8,128)(2,1)} %get-tuple-element.353, s32[]{:T(128)S(6)} %select_n.164), kind=kOutput, calls=%fused_computation.9.clone.1 | convolution fusion | flops 547356672 | bytes 9709572 | tf_op jit(solution)/shard_map/while/body/eval_jaxpr/igqp,pgd->igqd/dot_general | solution.py:102
  140.8 5.5 %bitcast_reduce_fusion.2 = (f32[128,16]{0,1:T(8,128)S(1)}, f32[1024,128,16]{1,0,2:T(8,128)}) fusion(pred[1024]{0:T(1024)(128)(4,1)S(1)} %add_compare_fusion.3, bf16[128,1,16,128]{3,0,2,1:T(8,128)(2,1)S(1)} %get-tuple-element.356, bf16[8,1024,2,1,128]{4,1,3,2,0:T(8,128)(2,1)} %get-tuple-element.353, s32[]{:T(128)S(6)} %select_n.164), kind=kOutput, calls=%fused_computation.2.clone.1 | convolution fusion | flops 543160320 | bytes 9184260 | tf_op jit(solution)/shard_map/while/body/eval_jaxpr/igqd,pgd->igqp/dot_general | solution.py:81
  147.0 5.8 %fusion.85 = f32[128,128,16]{1,0,2:T(8,128)S(1)} fusion(f32[1024,128,16]{1,0,2:T(8,128)} %get-tuple-element.311, f32[128,16]{0,1:T(8,128)S(1)} %max.47, pred[1024]{0:T(1024)(128)(4,1)S(1)} %add_compare_fusion.3, bf16[8,1024,2,1,128]{4,1,3,2,0:T(8,128)(2,1)} %get-tuple-element.353, s32[]{:T(128)S(6)} %select_n.164), kind=kOutput, calls=%fused_computation.9.clone.1 | convolution fusion | flops 547356672 | bytes 9709572 | tf_op jit(solution)/shard_map/while/body/eval_jaxpr/igqp,pgd->igqd/dot_general | solution.py:102
  160.8 5.5 %bitcast_reduce_fusion.2 = (f32[128,16]{0,1:T(8,128)S(1)}, f32[1024,128,16]{1,0,2:T(8,128)}) fusion(pred[1024]{0:T(1024)(128)(4,1)S(1)} %add_compare_fusion.3, bf16[128,1,16,128]{3,0,2,1:T(8,128)(2,1)S(1)} %get-tuple-element.356, bf16[8,1024,2,1,128]{4,1,3,2,0:T(8,128)(2,1)} %get-tuple-element.353, s32[]{:T(128)S(6)} %select_n.164), kind=kOutput, calls=%fused_computation.2.clone.1 | convolution fusion | flops 543160320 | bytes 9184260 | tf_op jit(solution)/shard_map/while/body/eval_jaxpr/igqd,pgd->igqp/dot_general | solution.py:81
  167.1 5.8 %fusion.85 = f32[128,128,16]{1,0,2:T(8,128)S(1)} fusion(f32[1024,128,16]{1,0,2:T(8,128)} %get-tuple-element.311, f32[128,16]{0,1:T(8,128)S(1)} %max.47, pred[1024]{0:T(1024)(128)(4,1)S(1)} %add_compare_fusion.3, bf16[8,1024,2,1,128]{4,1,3,2,0:T(8,128)(2,1)} %get-tuple-element.353, s32[]{:T(128)S(6)} %select_n.164), kind=kOutput, calls=%fused_computation.9.clone.1 | convolution fusion | flops 547356672 | bytes 9709572 | tf_op jit(solution)/shard_map/while/body/eval_jaxpr/igqp,pgd->igqd/dot_general | solution.py:102
  180.8 5.5 %bitcast_reduce_fusion.2 = (f32[128,16]{0,1:T(8,128)S(1)}, f32[1024,128,16]{1,0,2:T(8,128)}) fusion(pred[1024]{0:T(1024)(128)(4,1)S(1)} %add_compare_fusion.3, bf16[128,1,16,128]{3,0,2,1:T(8,128)(2,1)S(1)} %get-tuple-element.356, bf16[8,1024,2,1,128]{4,1,3,2,0:T(8,128)(2,1)} %get-tuple-element.353, s32[]{:T(128)S(6)} %select_n.164), kind=kOutput, calls=%fused_computation.2.clone.1 | convolution fusion | flops 543160320 | bytes 9184260 | tf_op jit(solution)/shard_map/while/body/eval_jaxpr/igqd,pgd->igqp/dot_general | solution.py:81
  187.1 5.8 %fusion.85 = f32[128,128,16]{1,0,2:T(8,128)S(1)} fusion(f32[1024,128,16]{1,0,2:T(8,128)} %get-tuple-element.311, f32[128,16]{0,1:T(8,128)S(1)} %max.47, pred[1024]{0:T(1024)(128)(4,1)S(1)} %add_compare_fusion.3, bf16[8,1024,2,1,128]{4,1,3,2,0:T(8,128)(2,1)} %get-tuple-element.353, s32[]{:T(128)S(6)} %select_n.164), kind=kOutput, calls=%fused_computation.9.clone.1 | convolution fusion | flops 547356672 | bytes 9709572 | tf_op jit(solution)/shard_map/while/body/eval_jaxpr/igqp,pgd->igqd/dot_general | solution.py:102
  200.9 5.5 %bitcast_reduce_fusion.2 = (f32[128,16]{0,1:T(8,128)S(1)}, f32[1024,128,16]{1,0,2:T(8,128)}) fusion(pred[1024]{0:T(1024)(128)(4,1)S(1)} %add_compare_fusion.3, bf16[128,1,16,128]{3,0,2,1:T(8,128)(2,1)S(1)} %get-tuple-element.356, bf16[8,1024,2,1,128]{4,1,3,2,0:T(8,128)(2,1)} %get-tuple-element.353, s32[]{:T(128)S(6)} %select_n.164), kind=kOutput, calls=%fused_computation.2.clone.1 | convolution fusion | flops 543160320 | bytes 9184260 | tf_op jit(solution)/shard_map/while/body/eval_jaxpr/igqd,pgd->igqp/dot_general | solution.py:81
  207.2 5.8 %fusion.85 = f32[128,128,16]{1,0,2:T(8,128)S(1)} fusion(f32[1024,128,16]{1,0,2:T(8,128)} %get-tuple-element.311, f32[128,16]{0,1:T(8,128)S(1)} %max.47, pred[1024]{0:T(1024)(128)(4,1)S(1)} %add_compare_fusion.3, bf16[8,1024,2,1,128]{4,1,3,2,0:T(8,128)(2,1)} %get-tuple-element.353, s32[]{:T(128)S(6)} %select_n.164), kind=kOutput, calls=%fused_computation.9.clone.1 | convolution fusion | flops 547356672 | bytes 9709572 | tf_op jit(solution)/shard_map/while/body/eval_jaxpr/igqp,pgd->igqd/dot_general | solution.py:102
  220.9 5.5 %bitcast_reduce_fusion.2 = (f32[128,16]{0,1:T(8,128)S(1)}, f32[1024,128,16]{1,0,2:T(8,128)}) fusion(pred[1024]{0:T(1024)(128)(4,1)S(1)} %add_compare_fusion.3, bf16[128,1,16,128]{3,0,2,1:T(8,128)(2,1)S(1)} %get-tuple-element.356, bf16[8,1024,2,1,128]{4,1,3,2,0:T(8,128)(2,1)} %get-tuple-element.353, s32[]{:T(128)S(6)} %select_n.164), kind=kOutput, calls=%fused_computation.2.clone.1 | convolution fusion | flops 543160320 | bytes 9184260 | tf_op jit(solution)/shard_map/while/body/eval_jaxpr/igqd,pgd->igqp/dot_general | solution.py:81
  227.2 5.8 %fusion.85 = f32[128,128,16]{1,0,2:T(8,128)S(1)} fusion(f32[1024,128,16]{1,0,2:T(8,128)} %get-tuple-element.311, f32[128,16]{0,1:T(8,128)S(1)} %max.47, pred[1024]{0:T(1024)(128)(4,1)S(1)} %add_compare_fusion.3, bf16[8,1024,2,1,128]{4,1,3,2,0:T(8,128)(2,1)} %get-tuple-element.353, s32[]{:T(128)S(6)} %select_n.164), kind=kOutput, calls=%fused_computation.9.clone.1 | convolution fusion | flops 547356672 | bytes 9709572 | tf_op jit(solution)/shard_map/while/body/eval_jaxpr/igqp,pgd->igqd/dot_general | solution.py:102
  237.2 4.8 %multiply_reduce_fusion = f32[128,16,128]{0,2,1:T(8,128)S(1)} fusion(f32[8,128,16,128]{1,3,2,0:T(8,128)} %get-tuple-element.146, f32[8,128,16]{1,2,0:T(8,128)S(1)} %get-tuple-element.224), kind=kLoop, calls=%fused_computation.47 | loop fusion | flops 3932160 | bytes 9502720 | tf_op jit(solution)/shard_map/reduce_sum | solution.py:126
  243.9 5.2 %all-to-all-start.1 = ((f32[4,32,2080]{2,1,0:T(8,128)}), f32[4,32,2080]{2,1,0:T(8,128)S(1)}, u32[]{:S(2)}, u32[]{:S(2)}) async-start(f32[4,32,2080]{2,1,0:T(8,128)} %concatenate.17), calls=%async_computation.1 | async-start | bytes 2228224 | tf_op jit(solution)/shard_map/all_to_all | solution.py:130
  250.3 13.1 %all-to-all-done.1 = f32[4,32,2080]{2,1,0:T(8,128)S(1)} async-done(((f32[4,32,2080]{2,1,0:T(8,128)}), f32[4,32,2080]{2,1,0:T(8,128)S(1)}, u32[]{:S(2)}, u32[]{:S(2)}) %all-to-all-start.1) | async-done | bytes 1064992 | tf_op jit(solution)/shard_map/all_to_all | solution.py:130
  (176 shorter events, 50.1 us)
Async XLA Ops:
  0.0 70.0 %copy-start = (bf16[32,128]{1,0:T(8,128)(2,1)S(1)}, bf16[32,128]{1,0:T(8,128)(2,1)}, u32[]{:S(2)}) copy-start(bf16[32,128]{1,0:T(8,128)(2,1)} %param.13) | copy-start | bytes 24580
  6.8 11.8 %copy-start.1 = (bf16[4,16384]{1,0:T(4,128)(2,1)S(1)}, bf16[4,16384]{1,0:T(4,128)(2,1)}, u32[]{:S(2)}) copy-start(bf16[4,16384]{1,0:T(4,128)(2,1)} %param.10) | copy-start | bytes 393220
  6.8 22.4 %copy-start.3 = (s32[8,128]{1,0:T(8,128)S(1)}, s32[8,128]{1,0:T(8,128)}, u32[]{:S(2)}) copy-start(s32[8,128]{1,0:T(8,128)} %param.15) | copy-start | bytes 12292
  6.8 24.6 %copy-start.4 = (s32[8]{0:T(128)S(1)}, s32[8]{0:T(128)}, u32[]{:S(2)}) copy-start(s32[8]{0:T(128)} %param.17) | copy-start | bytes 100
  11.0 59.2 %all-to-all-start = ((bf16[8,1024,256]{1,2,0:T(8,128)(2,1)}), bf16[8,1024,256]{1,2,0:T(8,128)(2,1)}, u32[]{:S(2)}, u32[]{:S(2)}) async-start(bf16[8,1024,256]{1,2,0:T(8,128)(2,1)} %pad_maximum_fusion), calls=%async_computation | async-start | bytes 8388608 | tf_op jit(solution)/shard_map/all_to_all | solution.py:63
  18.5 58.1 %copy-start.2 = (bf16[32,128]{1,0:T(8,128)(2,1)S(1)}, bf16[32,128]{1,0:T(8,128)(2,1)}, u32[]{:S(2)}) copy-start(bf16[32,128]{1,0:T(8,128)(2,1)} %param.14) | copy-start | bytes 24580
  18.6 13.5 %collective-permute-start = (bf16[4,2048]{1,0:T(4,128)(2,1)S(1)}, bf16[4,2048]{1,0:T(4,128)(2,1)S(1)}, u32[]{:S(2)}, u32[]{:S(2)}) collective-permute-start(bf16[4,2048]{1,0:T(4,128)(2,1)S(1)} %get-tuple-element.233), channel_id=1, source_target_pairs={{0,1},{1,0},{2,3},{3,2},{4,5},{5,4},{6,7},{7,6},{8,9},{9,8},{10,11... | collective-permute-start | bytes 49160 | tf_op jit(solution)/shard_map/ppermute | solution.py:57
  20.4 15.9 %collective-permute-start.1 = (bf16[4,2048]{1,0:T(4,128)(2,1)S(1)}, bf16[4,2048]{1,0:T(4,128)(2,1)S(1)}, u32[]{:S(2)}, u32[]{:S(2)}) collective-permute-start(bf16[4,2048]{1,0:T(4,128)(2,1)S(1)} %get-tuple-element.232), channel_id=1, source_target_pairs={{0,2},{1,3},{2,0},{3,1},{4,6},{5,7},{6,4},{7,5},{8,10},{9,11},{10,... | collective-permute-start | bytes 49160 | tf_op jit(solution)/shard_map/ppermute | solution.py:57
  23.4 13.0 %collective-permute-start.2 = (bf16[4,2048]{1,0:T(4,128)(2,1)S(1)}, bf16[4,2048]{1,0:T(4,128)(2,1)S(1)}, u32[]{:S(2)}, u32[]{:S(2)}) collective-permute-start(bf16[4,2048]{1,0:T(4,128)(2,1)S(1)} %get-tuple-element.231), channel_id=1, source_target_pairs={{0,3},{1,2},{2,1},{3,0},{4,7},{5,6},{6,5},{7,4},{8,11},{9,10},{10,... | collective-permute-start | bytes 49160 | tf_op jit(solution)/shard_map/ppermute | solution.py:57
  23.4 13.1 %collective-permute-start.3 = (bf16[4,2048]{1,0:T(4,128)(2,1)S(1)}, bf16[4,2048]{1,0:T(4,128)(2,1)S(1)}, u32[]{:S(2)}, u32[]{:S(2)}) collective-permute-start(bf16[4,2048]{1,0:T(4,128)(2,1)S(1)} %get-tuple-element.230), channel_id=1, source_target_pairs={{0,4},{1,5},{2,6},{3,7},{4,0},{5,1},{6,2},{7,3},{8,12},{9,13},{10,... | collective-permute-start | bytes 49160 | tf_op jit(solution)/shard_map/ppermute | solution.py:57
  29.2 7.3 %collective-permute-start.4 = (bf16[4,2048]{1,0:T(4,128)(2,1)S(1)}, bf16[4,2048]{1,0:T(4,128)(2,1)S(1)}, u32[]{:S(2)}, u32[]{:S(2)}) collective-permute-start(bf16[4,2048]{1,0:T(4,128)(2,1)S(1)} %get-tuple-element.229), channel_id=1, source_target_pairs={{0,5},{1,4},{2,7},{3,6},{4,1},{5,0},{6,3},{7,2},{8,13},{9,12},{10,... | collective-permute-start | bytes 49160 | tf_op jit(solution)/shard_map/ppermute | solution.py:57
  32.1 5.8 %collective-permute-start.5 = (bf16[4,2048]{1,0:T(4,128)(2,1)S(1)}, bf16[4,2048]{1,0:T(4,128)(2,1)S(1)}, u32[]{:S(2)}, u32[]{:S(2)}) collective-permute-start(bf16[4,2048]{1,0:T(4,128)(2,1)S(1)} %get-tuple-element.228), channel_id=1, source_target_pairs={{0,6},{1,7},{2,4},{3,5},{4,2},{5,3},{6,0},{7,1},{8,14},{9,15},{10,... | collective-permute-start | bytes 49160 | tf_op jit(solution)/shard_map/ppermute | solution.py:57
  36.3 4.3 %collective-permute-start.6 = (bf16[4,2048]{1,0:T(4,128)(2,1)S(1)}, bf16[4,2048]{1,0:T(4,128)(2,1)S(1)}, u32[]{:S(2)}, u32[]{:S(2)}) collective-permute-start(bf16[4,2048]{1,0:T(4,128)(2,1)S(1)} %get-tuple-element.227), channel_id=1, source_target_pairs={{0,7},{1,6},{2,5},{3,4},{4,3},{5,2},{6,1},{7,0},{8,15},{9,14},{10,... | collective-permute-start | bytes 49160 | tf_op jit(solution)/shard_map/ppermute | solution.py:57
  86.8 5.9 %slice-start = ((s8[8388608]{0:T(1024)(128)(4,1)}), s8[4194304]{0:T(1024)(128)(4,1)S(1)}, s32[]{:S(2)}) async-start(s8[8388608]{0:T(1024)(128)(4,1)} %bitcast.200), calls=%async_computation.2 | async-start | bytes 8388608 | tf_op jit(solution)/shard_map/while
  86.9 5.9 %slice-start.1 = ((s8[8388608]{0:T(1024)(128)(4,1)}), s8[4194304]{0:T(1024)(128)(4,1)S(1)}, s32[]{:S(2)}) async-start(s8[8388608]{0:T(1024)(128)(4,1)} %bitcast.200), calls=%async_computation.3 | async-start | bytes 8388608 | tf_op jit(solution)/shard_map/while
  106.8 5.9 %slice-start = ((s8[8388608]{0:T(1024)(128)(4,1)}), s8[4194304]{0:T(1024)(128)(4,1)S(1)}, s32[]{:S(2)}) async-start(s8[8388608]{0:T(1024)(128)(4,1)} %bitcast.200), calls=%async_computation.2 | async-start | bytes 8388608 | tf_op jit(solution)/shard_map/while
  106.9 5.9 %slice-start.1 = ((s8[8388608]{0:T(1024)(128)(4,1)}), s8[4194304]{0:T(1024)(128)(4,1)S(1)}, s32[]{:S(2)}) async-start(s8[8388608]{0:T(1024)(128)(4,1)} %bitcast.200), calls=%async_computation.3 | async-start | bytes 8388608 | tf_op jit(solution)/shard_map/while
  126.9 5.9 %slice-start = ((s8[8388608]{0:T(1024)(128)(4,1)}), s8[4194304]{0:T(1024)(128)(4,1)S(1)}, s32[]{:S(2)}) async-start(s8[8388608]{0:T(1024)(128)(4,1)} %bitcast.200), calls=%async_computation.2 | async-start | bytes 8388608 | tf_op jit(solution)/shard_map/while
  127.0 5.9 %slice-start.1 = ((s8[8388608]{0:T(1024)(128)(4,1)}), s8[4194304]{0:T(1024)(128)(4,1)S(1)}, s32[]{:S(2)}) async-start(s8[8388608]{0:T(1024)(128)(4,1)} %bitcast.200), calls=%async_computation.3 | async-start | bytes 8388608 | tf_op jit(solution)/shard_map/while
  146.9 5.9 %slice-start = ((s8[8388608]{0:T(1024)(128)(4,1)}), s8[4194304]{0:T(1024)(128)(4,1)S(1)}, s32[]{:S(2)}) async-start(s8[8388608]{0:T(1024)(128)(4,1)} %bitcast.200), calls=%async_computation.2 | async-start | bytes 8388608 | tf_op jit(solution)/shard_map/while
  147.0 5.9 %slice-start.1 = ((s8[8388608]{0:T(1024)(128)(4,1)}), s8[4194304]{0:T(1024)(128)(4,1)S(1)}, s32[]{:S(2)}) async-start(s8[8388608]{0:T(1024)(128)(4,1)} %bitcast.200), calls=%async_computation.3 | async-start | bytes 8388608 | tf_op jit(solution)/shard_map/while
  167.0 5.9 %slice-start = ((s8[8388608]{0:T(1024)(128)(4,1)}), s8[4194304]{0:T(1024)(128)(4,1)S(1)}, s32[]{:S(2)}) async-start(s8[8388608]{0:T(1024)(128)(4,1)} %bitcast.200), calls=%async_computation.2 | async-start | bytes 8388608 | tf_op jit(solution)/shard_map/while
  167.1 5.9 %slice-start.1 = ((s8[8388608]{0:T(1024)(128)(4,1)}), s8[4194304]{0:T(1024)(128)(4,1)S(1)}, s32[]{:S(2)}) async-start(s8[8388608]{0:T(1024)(128)(4,1)} %bitcast.200), calls=%async_computation.3 | async-start | bytes 8388608 | tf_op jit(solution)/shard_map/while
  187.0 5.9 %slice-start = ((s8[8388608]{0:T(1024)(128)(4,1)}), s8[4194304]{0:T(1024)(128)(4,1)S(1)}, s32[]{:S(2)}) async-start(s8[8388608]{0:T(1024)(128)(4,1)} %bitcast.200), calls=%async_computation.2 | async-start | bytes 8388608 | tf_op jit(solution)/shard_map/while
  187.1 5.9 %slice-start.1 = ((s8[8388608]{0:T(1024)(128)(4,1)}), s8[4194304]{0:T(1024)(128)(4,1)S(1)}, s32[]{:S(2)}) async-start(s8[8388608]{0:T(1024)(128)(4,1)} %bitcast.200), calls=%async_computation.3 | async-start | bytes 8388608 | tf_op jit(solution)/shard_map/while
  207.1 5.9 %slice-start = ((s8[8388608]{0:T(1024)(128)(4,1)}), s8[4194304]{0:T(1024)(128)(4,1)S(1)}, s32[]{:S(2)}) async-start(s8[8388608]{0:T(1024)(128)(4,1)} %bitcast.200), calls=%async_computation.2 | async-start | bytes 8388608 | tf_op jit(solution)/shard_map/while
  207.1 5.9 %slice-start.1 = ((s8[8388608]{0:T(1024)(128)(4,1)}), s8[4194304]{0:T(1024)(128)(4,1)S(1)}, s32[]{:S(2)}) async-start(s8[8388608]{0:T(1024)(128)(4,1)} %bitcast.200), calls=%async_computation.3 | async-start | bytes 8388608 | tf_op jit(solution)/shard_map/while
  227.1 5.9 %slice-start = ((s8[8388608]{0:T(1024)(128)(4,1)}), s8[4194304]{0:T(1024)(128)(4,1)S(1)}, s32[]{:S(2)}) async-start(s8[8388608]{0:T(1024)(128)(4,1)} %bitcast.200), calls=%async_computation.2 | async-start | bytes 8388608 | tf_op jit(solution)/shard_map/while
  227.2 5.9 %slice-start.1 = ((s8[8388608]{0:T(1024)(128)(4,1)}), s8[4194304]{0:T(1024)(128)(4,1)S(1)}, s32[]{:S(2)}) async-start(s8[8388608]{0:T(1024)(128)(4,1)} %bitcast.200), calls=%async_computation.3 | async-start | bytes 8388608 | tf_op jit(solution)/shard_map/while
  237.2 11.9 %copy-start.5 = (s32[8]{0:T(128)S(1)}, s32[8]{0:T(128)}, u32[]{:S(2)}) copy-start(s32[8]{0:T(128)} %param.16) | copy-start | bytes 100
  243.9 19.5 %all-to-all-start.1 = ((f32[4,32,2080]{2,1,0:T(8,128)}), f32[4,32,2080]{2,1,0:T(8,128)S(1)}, u32[]{:S(2)}, u32[]{:S(2)}) async-start(f32[4,32,2080]{2,1,0:T(8,128)} %concatenate.17), calls=%async_computation.1 | async-start | bytes 2228224 | tf_op jit(solution)/shard_map/all_to_all | solution.py:130
